TPU v7x, 128 devices: a whole 4x4x4 slice. The times are simulated.
128 devices in a mesh: row: 16 (over y, x), col: 8 (over z, core).
Axes of the slice: x: 4, y: 4, z: 4, core: 2. Of those that a mesh axis runs over, the one named last changes fastest.
Arguments:
- amplitudes: bfloat16 [16384, 3072], P(('row', 'col')), may hold values from -6 to 6
- integrals: bfloat16 [8, 3072, 9600], P('col', None, 'row'), may hold values from -0.109375 to 0.109375
- irreps: int32 [16384], P(('row', 'col')), may hold values from 0 to 7, as said below
- row_mirror: int32 [16384], P(('row', 'col')), may hold values from 0 to 127, as said below
- col_mirror: int32 [9600], replicated, may hold values from 0 to 9599, as said below
Outputs:
- symmetrized: bfloat16 [16384, 9600], P(('row', 'col'))
Inputs may be any that keep to these rules, and one draw needn't show every extreme that they name: `irreps`: among the 128 pairs of one block, no irrep occurs more than 32 times; in every block one irrep, the same for all blocks, occurs exactly 32 times. A pair and its mirrored partner have the same irrep. `row_mirror`: within each block of 128 pairs the map is an involution without fixed points. `col_mirror`: an involution of the 9600 slab columns without fixed points.
All inputs are finite; a program needn't handle non-finite values.
Results may differ from a plain program's by a relative error of at most 0.0051.
Values may be sent and summed in bfloat16 or wider, within the bound.
A program may use at most 192 MiB of HBM per device.

v0:
```python
import jax
import jax.numpy as jnp
from jax import lax
from jax.sharding import PartitionSpec as P

IRREPS = 8


def body(amplitudes, integrals, irreps, row_mirror, col_mirror):
    pair_count = amplitudes.shape[0]
    contract = amplitudes.shape[1]
    col_count = lax.axis_size("col")
    per_owner = integrals.shape[0]
    capacity = pair_count // 4
    onehot = (irreps[:, None] == jnp.arange(IRREPS, dtype=jnp.int32)[None, :]).astype(jnp.int32)
    before = jnp.cumsum(onehot, axis=0) - onehot
    slot_index = jnp.sum(before * onehot, axis=1)
    owner_col = irreps // per_owner
    within = irreps % per_owner
    position = within * (col_count * capacity) + owner_col * capacity + slot_index
    outgoing = (
        jnp.zeros((per_owner * col_count * capacity, contract), jnp.bfloat16)
        .at[position]
        .set(amplitudes)
    )
    outgoing = outgoing.reshape(per_owner, col_count, capacity, contract)
    arrived = lax.all_to_all(outgoing, "col", split_axis=1, concat_axis=1, tiled=True)
    arrived = arrived.reshape(per_owner, col_count * capacity, contract)
    shares = jnp.einsum(
        "irk,iks->irs",
        lax.all_gather(arrived, "row", axis=1, tiled=True),
        integrals,
        preferred_element_type=jnp.float32,
    ).astype(jnp.bfloat16)
    result = lax.all_to_all(shares, "row", split_axis=1, concat_axis=2, tiled=True)
    slab_width = result.shape[2]
    result = result.reshape(per_owner, col_count, capacity, slab_width)
    returned = lax.all_to_all(result, "col", split_axis=1, concat_axis=1, tiled=True)
    ladder = returned.reshape(per_owner * col_count * capacity, slab_width)[position]
    mirrored = ladder[row_mirror][:, col_mirror]
    return (ladder.astype(jnp.float32) + mirrored.astype(jnp.float32)).astype(jnp.bfloat16)


def solution(mesh):
    return jax.shard_map(
        body,
        mesh=mesh,
        in_specs=(
            P(("row", "col"), None),
            P("col", None, "row"),
            P(("row", "col")),
            P(("row", "col")),
            P(),
        ),
        out_specs=P(("row", "col"), None),
        check_vma=False,
    )
```

profile of v0, /device:TPU:1, one launch (start us, length us, event | category | flops | bytes accessed | tf_op | source)
XLA Modules:
  0.0 593.4 jit_solution(5129053764023563648)
XLA Ops:
  6.5 0.7 fusion.12
  7.5 0.8 select_reduce_fusion
  8.3 0.7 compare_select_fusion.2
  9.0 2.8 scatter_custom_fusion
  11.8 27.5 %all_to_all.25 = bf16[1,8,32,3072]{3,2,0,1:T(8,128)(2,1)} all-to-all(bf16[1,8,32,3072]{3,2,0,1:T(8,128)(2,1)S(1)} %bitcast.34), channel_id=1, replica_groups=mesh['row'=16,'col'=8] {'col'}, dimensions={1} | all-to-all | bytes 3145728 | tf_op jit(solution)/shard_map/all_to_all | solution.py:27
  39.3 154.1 %all-gather.2.cloned.1.call-done = bf16[1,4096,3072]{2,1,0:T(8,128)(2,1)} async-done(((bf16[1,256,3072]{2,1,0:T(8,128)(2,1)}), bf16[1,4096,3072]{2,1,0:T(8,128)(2,1)}) %all-gather.2.cloned.1.call-update) | async-done | bytes 25165840 | tf_op jit(solution)/shard_map/all_gather | solution.py:31
  193.4 22.7 %fusion.5 = bf16[1,4096,600]{1,2,0:T(8,128)(2,1)} fusion(bf16[1,4096,3072]{2,1,0:T(8,128)(2,1)} %all-gather.2.cloned.1.call-done, bf16[1,3072,600]{1,2,0:T(8,128)(2,1)} %param.6), kind=kOutput, calls=%fused_computation.7 | convolution fusion | flops 15101952000 | bytes 33767424 | tf_op jit(solution)/shard_map/irk,iks->irs/dot_general | solution.py:29
  216.0 21.3 %copy.18 = bf16[1,4096,600]{2,0,1:T(2,128)(2,1)} copy(bf16[1,4096,600]{1,2,0:T(8,128)(2,1)} %fusion.5) | data formatting | bytes 9830400 | tf_op jit(solution)/shard_map/convert_element_type | solution.py:34
  237.8 113.4 %reduce = bf16[4096,600]{1,0:T(8,128)(2,1)} reduce(bf16[4096,1,600]{2,1,0:T(2,128)(2,1)} %bitcast.28, bf16[]{:T(256)} %broadcast.43), dimensions={1}, to_apply=%bitcast.26.reduce_sub_computation | reduce | bytes 9830402
  351.2 14.9 %reshape.67 = bf16[16,2,76800]{2,1,0:T(2,128)(2,1)} reshape(bf16[4096,600]{1,0:T(8,128)(2,1)} %reduce) | data formatting | bytes 9830400
  366.1 62.8 %all_to_all.26 = bf16[16,2,76800]{2,1,0:T(2,128)(2,1)} all-to-all(bf16[16,2,76800]{2,1,0:T(2,128)(2,1)} %reshape.67), channel_id=1, replica_groups=mesh['row'=16,'col'=8] {'row'}, dimensions={0} | all-to-all | bytes 9830400 | tf_op jit(solution)/shard_map/all_to_all | solution.py:35
  428.9 16.1 %reshape.68 = bf16[4096,1,600]{2,1,0:T(2,128)(2,1)} reshape(bf16[16,2,76800]{2,1,0:T(2,128)(2,1)} %all_to_all.26) | data formatting | bytes 9830400
  445.0 7.2 %copy.25 = bf16[1,4096,600]{2,1,0:T(8,128)(2,1)} copy(bf16[1,4096,600]{2,0,1:T(2,128)(2,1)} %bitcast.29) | data formatting | bytes 9830400
  452.2 8.6 %copy.24 = bf16[1,16,256,600]{2,1,3,0:T(8,128)(2,1)} copy(bf16[1,16,256,600]{3,2,1,0:T(8,128)(2,1)} %bitcast.30) | data formatting | bytes 9830400 | tf_op jit(solution)/shard_map/all_to_all | solution.py:35
  460.8 9.5 %copy.20 = bf16[1,256,16,600]{3,2,1,0:T(8,128)(2,1)} copy(bf16[1,256,16,600]{1,2,3,0:T(8,128)(2,1)} %bitcast.32) | data formatting | bytes 9830400 | tf_op jit(solution)/shard_map/all_to_all | solution.py:35
  470.3 9.1 %reshape.26 = bf16[1,8,32,9600]{3,2,1,0:T(8,128)(2,1)} reshape(bf16[1,256,16,600]{3,2,1,0:T(8,128)(2,1)} %copy.20) | data formatting | bytes 9830400 | tf_op jit(solution)/shard_map/reshape | solution.py:37
  479.4 6.4 %all-to-all-start.2 = ((bf16[1,8,32,9600]{3,2,0,1:T(8,128)(2,1)}), bf16[1,8,32,9600]{3,2,0,1:T(8,128)(2,1)}, u32[]{:S(2)}, u32[]{:S(2)}) async-start(bf16[1,8,32,9600]{3,2,0,1:T(8,128)(2,1)} %bitcast.31), calls=%async_computation.2 | async-start | bytes 9830400 | tf_op jit(solution)/shard_map/all_to_all | solution.py:38
  485.9 56.6 %all-to-all-done.2 = bf16[1,8,32,9600]{3,2,0,1:T(8,128)(2,1)} async-done(((bf16[1,8,32,9600]{3,2,0,1:T(8,128)(2,1)}), bf16[1,8,32,9600]{3,2,0,1:T(8,128)(2,1)}, u32[]{:S(2)}, u32[]{:S(2)}) %all-to-all-start.2) | async-done | bytes 4915232 | tf_op jit(solution)/shard_map/all_to_all | solution.py:38
  542.5 7.5 %gather_fusion = bf16[128,9600]{1,0:T(8,128)(2,1)S(1)} fusion(bf16[256,9600]{1,0:T(8,128)(2,1)} %bitcast.8, s32[1024]{0:T(1024)S(1)} %pad_clamp_fusion.2), kind=kCustom, calls=%fused_computation | custom fusion | bytes 4915712 | tf_op jit(solution)/shard_map/gather | solution.py:39
  550.0 3.5 gather_fusion.1
  553.5 4.3 copy.22
  557.9 20.7 %gather_fusion.2 = bf16[9600,128]{1,0:T(8,128)(2,1)} fusion(bf16[128,9600]{0,1:T(8,128)(2,1)} %copy.22, s32[10240]{0:T(1024)S(1)} %pad_clamp_fusion), kind=kCustom, calls=%fused_computation.2 | custom fusion | bytes 4953600 | tf_op jit(solution)/shard_map/gather | solution.py:40
  578.5 4.4 copy.23
  582.9 3.7 fusion.8
  (13 shorter events, 0.7 us)
Async XLA Ops:
  6.5 186.8 %all-gather.2.cloned.1.call-start = ((), (), s32[]{:S(2)}) async-start(), calls=%async_computation.3 | async-start | bytes 26738688 | tf_op jit(solution)/shard_map/all_gather | solution.py:31
  479.4 6.5 %copy-start.1 = (s32[128]{0:T(128)S(1)}, s32[128]{0:T(128)}, u32[]{:S(2)}) copy-start(s32[128]{0:T(128)} %param.8) | copy-start | bytes 1540
  479.4 6.5 %copy-start = (s32[9600]{0:T(1024)S(1)}, s32[9600]{0:T(1024)}, u32[]{:S(2)}) copy-start(s32[9600]{0:T(1024)} %param.9) | copy-start | bytes 115204
  479.4 63.1 %all-to-all-start.2 = ((bf16[1,8,32,9600]{3,2,0,1:T(8,128)(2,1)}), bf16[1,8,32,9600]{3,2,0,1:T(8,128)(2,1)}, u32[]{:S(2)}, u32[]{:S(2)}) async-start(bf16[1,8,32,9600]{3,2,0,1:T(8,128)(2,1)} %bitcast.31), calls=%async_computation.2 | async-start | bytes 9830400 | tf_op jit(solution)/shard_map/all_to_all | solution.py:38
Sparse Core Ops, SparseCore 0:
  39.4 153.9 all-gather.1
where the time goes:
time: 596 us; the launch traced here: 593 us
  waiting for transfers between devices  211 us (35%)
  local copies, waits for them, and re-layouts  130 us (22%)
  other arithmetic  119 us (20%)
  blocking collectives  90.3 us (15%)
  matrix products  22.7 us (4%)
  between operations  13.5 us (2%)
  starting transfers between devices  6.45 us (1%)
    all_gather x1, waiting for transfers between devices, body(): lax.all_gather(arrived, 'row', axis=1, tiled=True)  154 us
    unnamed x1, other arithmetic  113 us
    all_to_all x1, blocking collectives, body(): lax.all_to_all(shares, 'row', split_axis=1, concat_axis=2, tiled=True)  62.8 us
    all_to_all x1, waiting for transfers between devices, body(): lax.all_to_all(result, 'col', split_axis=1, concat_axis=1, tiled=True)  56.6 us
    unnamed x8, local copies, waits for them, and re-layouts  38.7 us
    gather x4, local copies, waits for them, and re-layouts, body(): mirrored = ladder[row_mirror][:, col_mirror]  32.9 us
    all_to_all x1, blocking collectives, body(): lax.all_to_all(outgoing, 'col', split_axis=1, concat_axis=1, tiled=True)  27.5 us
    dot_general x1, matrix products, body(): jnp.einsum('irk,iks->irs', lax.all_gather(arrived, 'row', axis=1, tiled=T...  22.7 us
  transfers between devices with their start and end apart: 2, of which 2 were waited for; matrix products, arithmetic and copies ran while one was open for 0% of the time, Pallas kernels for 0%

commit v1 on v0

--- a/solution.py
+++ b/solution.py
@@ -4,6 +4,11 @@
 from jax.sharding import PartitionSpec as P
 
 IRREPS = 8
+
+
+def exchange_gather(x, axis, dim):
+    outgoing = jnp.stack([x] * lax.axis_size(axis))
+    return jnp.concatenate(lax.all_to_all(outgoing, axis, 0, 0), axis=dim)
 
 
 def body(amplitudes, integrals, irreps, row_mirror, col_mirror):
@@ -28,7 +33,7 @@
     arrived = arrived.reshape(per_owner, col_count * capacity, contract)
     shares = jnp.einsum(
         "irk,iks->irs",
-        lax.all_gather(arrived, "row", axis=1, tiled=True),
+        exchange_gather(arrived, "row", 1),
         integrals,
         preferred_element_type=jnp.float32,
     ).astype(jnp.bfloat16)

time: 596 us -> 713 us (1.20)
  blocking collectives: 90.3 us -> 371 us
  waiting for transfers between devices: 211 us -> 56.6 us
  between operations: 13.5 us -> 0.11 us
    all_to_all x0 -> x1, blocking collectives: none -> 281 us  [exchange_gather(): return jnp.concatenate(lax.all_to_all(outgoing, axis, 0, 0), axis=dim)]
    all_gather x1 -> x0, waiting for transfers between devices: 154 us -> none  [body(): lax.all_gather(arrived, 'row', axis=1, tiled=True)]
    unnamed x8 -> x10, local copies, waits for them, and re-layouts: 38.7 us -> 38.7 us
  transfers between devices with their start and end apart: 2 -> 1, of which waited for: 2 -> 1; matrix products, arithmetic and copies ran while one was open for 0% -> 0% of each run, Pallas kernels for 0% -> 0%
where the time goes in v1:
time: 713 us; the launch traced here: 710 us
  blocking collectives  371 us (52%)
  local copies, waits for them, and re-layouts  134 us (19%)
  other arithmetic  119 us (17%)
  waiting for transfers between devices  56.6 us (8%)
  matrix products  21.6 us (3%)
  starting transfers between devices  7.79 us (1%)
    all_to_all x1, blocking collectives, exchange_gather(): return jnp.concatenate(lax.all_to_all(outgoing, axis, 0, 0), axis=dim)  281 us
    unnamed x1, other arithmetic  113 us
    all_to_all x1, blocking collectives, body(): lax.all_to_all(shares, 'row', split_axis=1, concat_axis=2, tiled=True)  62.3 us
    all_to_all x1, waiting for transfers between devices, body(): lax.all_to_all(result, 'col', split_axis=1, concat_axis=1, tiled=True)  56.6 us
    unnamed x10, local copies, waits for them, and re-layouts  38.7 us
    gather x4, local copies, waits for them, and re-layouts, body(): mirrored = ladder[row_mirror][:, col_mirror]  32.9 us
    all_to_all x1, blocking collectives, body(): lax.all_to_all(outgoing, 'col', split_axis=1, concat_axis=1, tiled=True)  27.4 us
    dot_general x1, matrix products, body(): jnp.einsum('irk,iks->irs', exchange_gather(arrived, 'row', 1), integrals,...  21.6 us
  transfers between devices with their start and end apart: 1, of which 1 were waited for; matrix products, arithmetic and copies ran while one was open for 0% of the time, Pallas kernels for 0%

profile of v1, /device:TPU:1, one launch (start us, length us, event | category | flops | bytes accessed | tf_op | source)
XLA Modules:
  0.0 710.1 jit_solution(12568564353023716739)
XLA Ops:
  0.0 0.7 fusion.5
  0.9 0.8 select_reduce_fusion
  2.4 2.8 scatter_custom_fusion
  5.2 27.4 %all_to_all.30 = bf16[1,8,32,3072]{3,2,0,1:T(8,128)(2,1)S(1)} all-to-all(bf16[1,8,32,3072]{3,2,0,1:T(8,128)(2,1)S(1)} %bitcast.29), channel_id=1, replica_groups=mesh['row'=16,'col'=8] {'col'}, dimensions={1} | all-to-all | bytes 3145728 | tf_op jit(solution)/shard_map/all_to_all | solution.py:32
  32.6 3.2 stack.3
  35.8 281.2 %all_to_all.31 = bf16[16,1,256,3072]{3,2,1,0:T(8,128)(2,1)} all-to-all(bf16[16,1,256,3072]{3,2,1,0:T(8,128)(2,1)S(1)} %stack.3), channel_id=1, replica_groups=mesh['row'=16,'col'=8] {'row'}, dimensions={0} | all-to-all | bytes 50331648 | tf_op jit(solution)/shard_map/all_to_all | solution.py:11
  317.1 21.6 %fusion = bf16[1,4096,600]{1,2,0:T(8,128)(2,1)} fusion(bf16[4096,3072]{1,0:T(8,128)(2,1)} %bitcast.25, bf16[1,3072,600]{1,2,0:T(8,128)(2,1)S(1)} %copy-done.1), kind=kOutput, calls=%fused_computation.5 | convolution fusion | flops 15101952000 | bytes 33767424 | tf_op jit(solution)/shard_map/irk,iks->irs/dot_general | solution.py:34
  338.7 21.3 %copy.18 = bf16[1,4096,600]{2,0,1:T(2,128)(2,1)} copy(bf16[1,4096,600]{1,2,0:T(8,128)(2,1)} %fusion) | data formatting | bytes 9830400 | tf_op jit(solution)/shard_map/convert_element_type | solution.py:39
  360.5 113.4 %reduce = bf16[4096,600]{1,0:T(8,128)(2,1)} reduce(bf16[4096,1,600]{2,1,0:T(2,128)(2,1)} %bitcast.23, bf16[]{:T(256)} %broadcast.45), dimensions={1}, to_apply=%bitcast.20.reduce_sub_computation | reduce | bytes 9830402
  473.8 14.9 %reshape.69 = bf16[16,2,76800]{2,1,0:T(2,128)(2,1)} reshape(bf16[4096,600]{1,0:T(8,128)(2,1)} %reduce) | data formatting | bytes 9830400
  488.8 62.3 %all_to_all.32 = bf16[16,2,76800]{2,1,0:T(2,128)(2,1)} all-to-all(bf16[16,2,76800]{2,1,0:T(2,128)(2,1)} %reshape.69), channel_id=1, replica_groups=mesh['row'=16,'col'=8] {'row'}, dimensions={0} | all-to-all | bytes 9830400 | tf_op jit(solution)/shard_map/all_to_all | solution.py:40
  551.1 16.1 %reshape.70 = bf16[4096,1,600]{2,1,0:T(2,128)(2,1)} reshape(bf16[16,2,76800]{2,1,0:T(2,128)(2,1)} %all_to_all.32) | data formatting | bytes 9830400
  567.2 7.2 %copy.25 = bf16[1,4096,600]{2,1,0:T(8,128)(2,1)} copy(bf16[1,4096,600]{2,0,1:T(2,128)(2,1)} %bitcast.24) | data formatting | bytes 9830400
  574.4 8.6 %copy.24 = bf16[1,16,256,600]{2,1,3,0:T(8,128)(2,1)} copy(bf16[1,16,256,600]{3,2,1,0:T(8,128)(2,1)} %bitcast.26) | data formatting | bytes 9830400 | tf_op jit(solution)/shard_map/all_to_all | solution.py:40
  583.0 9.5 %copy.20 = bf16[1,256,16,600]{3,2,1,0:T(8,128)(2,1)} copy(bf16[1,256,16,600]{1,2,3,0:T(8,128)(2,1)} %bitcast.28) | data formatting | bytes 9830400 | tf_op jit(solution)/shard_map/all_to_all | solution.py:40
  592.5 9.1 %reshape.28 = bf16[1,8,32,9600]{3,2,1,0:T(8,128)(2,1)} reshape(bf16[1,256,16,600]{3,2,1,0:T(8,128)(2,1)} %copy.20) | data formatting | bytes 9830400 | tf_op jit(solution)/shard_map/reshape | solution.py:42
  601.6 7.8 %all-to-all-start.3 = ((bf16[1,8,32,9600]{3,2,0,1:T(8,128)(2,1)}), bf16[1,8,32,9600]{3,2,0,1:T(8,128)(2,1)}, u32[]{:S(2)}, u32[]{:S(2)}) async-start(bf16[1,8,32,9600]{3,2,0,1:T(8,128)(2,1)} %bitcast.27), calls=%async_computation.3 | async-start | bytes 9830400 | tf_op jit(solution)/shard_map/all_to_all | solution.py:43
  609.5 56.6 %all-to-all-done.3 = bf16[1,8,32,9600]{3,2,0,1:T(8,128)(2,1)} async-done(((bf16[1,8,32,9600]{3,2,0,1:T(8,128)(2,1)}), bf16[1,8,32,9600]{3,2,0,1:T(8,128)(2,1)}, u32[]{:S(2)}, u32[]{:S(2)}) %all-to-all-start.3) | async-done | bytes 4915232 | tf_op jit(solution)/shard_map/all_to_all | solution.py:43
  666.0 7.5 %gather_fusion = bf16[128,9600]{1,0:T(8,128)(2,1)S(1)} fusion(bf16[256,9600]{1,0:T(8,128)(2,1)} %bitcast.8, s32[1024]{0:T(1024)S(1)} %pad_clamp_fusion.2), kind=kCustom, calls=%fused_computation | custom fusion | bytes 4915712 | tf_op jit(solution)/shard_map/gather | solution.py:44
  673.5 3.5 gather_fusion.1
  677.1 4.3 copy.22
  681.4 20.7 %gather_fusion.2 = bf16[9600,128]{1,0:T(8,128)(2,1)} fusion(bf16[128,9600]{0,1:T(8,128)(2,1)} %copy.22, s32[10240]{0:T(1024)S(1)} %pad_clamp_fusion), kind=kCustom, calls=%fused_computation.2 | custom fusion | bytes 4953600 | tf_op jit(solution)/shard_map/gather | solution.py:45
  702.1 4.4 copy.23
  706.4 3.7 fusion.1
  (14 shorter events, 1.4 us)
Async XLA Ops:
  35.8 281.3 %copy-start.1 = (bf16[1,3072,600]{1,2,0:T(8,128)(2,1)S(1)}, bf16[1,3072,600]{1,2,0:T(8,128)(2,1)}, u32[]{:S(2)}) copy-start(bf16[1,3072,600]{1,2,0:T(8,128)(2,1)} %param.6) | copy-start | bytes 11059204
  601.6 7.8 %copy-start.2 = (s32[128]{0:T(128)S(1)}, s32[128]{0:T(128)}, u32[]{:S(2)}) copy-start(s32[128]{0:T(128)} %param.8) | copy-start | bytes 1540
  601.6 7.8 %copy-start = (s32[9600]{0:T(1024)S(1)}, s32[9600]{0:T(1024)}, u32[]{:S(2)}) copy-start(s32[9600]{0:T(1024)} %param.9) | copy-start | bytes 115204
  601.6 64.4 %all-to-all-start.3 = ((bf16[1,8,32,9600]{3,2,0,1:T(8,128)(2,1)}), bf16[1,8,32,9600]{3,2,0,1:T(8,128)(2,1)}, u32[]{:S(2)}, u32[]{:S(2)}) async-start(bf16[1,8,32,9600]{3,2,0,1:T(8,128)(2,1)} %bitcast.27), calls=%async_computation.3 | async-start | bytes 9830400 | tf_op jit(solution)/shard_map/all_to_all | solution.py:43
